TPU v7x, 256 devices: a whole 4x4x8 slice. The times are simulated.
256 devices in a mesh: row: 16 (over z, core), col: 16 (over x, y).
Axes of the slice: x: 4, y: 4, z: 8, core: 2. Of those that a mesh axis runs over, the one named last changes fastest.
Arguments:
- factor: float32 [1, 16, 896, 1, 16, 896], P(None, 'row', None, None, 'col'), as said below
- damping: float32 [1], replicated, may hold values from 0.1 to 1
Outputs:
- factor_state: float32 [1, 16, 896, 1, 16, 896], P(None, 'row', None, None, 'col')
Inputs may be any that keep to these rules, and one draw needn't show every extreme that they name: factor is symmetric and positive semidefinite, so that A's smallest eigenvalue is at least damping[0].
All inputs are finite; a program needn't handle non-finite values.
Results may differ from a plain program's by a relative error of at most 0.00016.
Values sent between devices are 32-bit elements; how exact they have to be, the bound alone decides.
No kernel may reach another device: no remote copies, remote signals or barrier semaphores. Data moves between devices by JAX's collectives and lax.ppermute only.
A program may use at most 128 MiB of HBM per device.

v0:
```python
import jax
import jax.numpy as jnp
from jax import lax
from jax.sharding import PartitionSpec as P


def broadcast(array, axis, root):
    mine = lax.axis_index(axis) == root
    return lax.psum(jnp.where(mine, array, jnp.zeros_like(array)), axis)


def times_transposed(left, right):
    return lax.dot_general(
        left,
        right,
        (((1,), (1,)), ((), ())),
        precision=lax.Precision.HIGHEST,
        preferred_element_type=jnp.float32,
    )


def on_device(factor, damping):
    grid_rows = lax.axis_size("row")
    grid_cols = lax.axis_size("col")
    row_index = lax.axis_index("row")
    col_index = lax.axis_index("col")
    tile_rows = factor.shape[0]
    tile_cols = factor.shape[3]
    tile_order = factor.shape[2]
    strip_rows = tile_order // grid_cols
    first_axis = lax.broadcasted_iota(jnp.int32, (tile_order, tile_order), 0)
    second_axis = lax.broadcasted_iota(jnp.int32, (tile_order, tile_order), 1)
    identity = (first_axis == second_axis).astype(jnp.float32)
    empty = jnp.zeros((tile_order, tile_order), jnp.float32)
    row_ids = [0 + row_index]
    col_ids = [0 + col_index]
    tiles = [
        [factor[0, 0, :, 0, 0, :] + jnp.where(row_ids[0] == col_ids[0], damping[0], 0.0) * identity]
    ]

    def factor_tile(square):
        lower = jnp.linalg.cholesky(square)
        return (lower, jax.scipy.linalg.solve_triangular(lower, identity, lower=True))

    def skip_factor(square):
        return (empty, empty)

    def solve_all(blocks, inverse):
        return jnp.stack([times_transposed(blocks[0], inverse)])

    def solve_none(blocks, inverse):
        return jnp.zeros_like(blocks)

    panels = []

    def apply_panel(square, row_slot, col_slot, panel_id):
        return square - times_transposed(
            panels[panel_id][0][row_slot], panels[panel_id][1][col_slot]
        )

    home_row = 0 % grid_rows
    home_col = 0 % grid_cols
    slot_row = 0 // grid_rows
    slot_col = 0 // grid_cols
    is_home = jnp.logical_and(row_index == home_row, col_index == home_col)
    in_panel = col_index == home_col
    diag_lower, diag_inverse = lax.cond(
        is_home, factor_tile, skip_factor, tiles[slot_row][slot_col]
    )
    own_blocks = jnp.stack([tiles[0][slot_col]])
    inverse_here = broadcast(diag_inverse, "row", home_row)
    solved_own = lax.cond(in_panel, solve_all, solve_none, own_blocks, inverse_here)
    outgoing = jnp.stack(
        [jnp.where(row_ids[0] > 0, solved_own[0], jnp.where(row_ids[0] == 0, diag_lower, 0.0))]
    )
    strips = lax.all_to_all(outgoing, "col", split_axis=1, concat_axis=1, tiled=True)
    home_strip = lax.slice_in_dim(
        strips, home_col * strip_rows, (home_col + 1) * strip_rows, axis=1
    )
    arrived = lax.all_gather(home_strip, "col", axis=1, tiled=True)
    row_slot = 0
    tiles[row_slot][slot_col] = jnp.where(in_panel, arrived[row_slot], tiles[row_slot][slot_col])
    col_slot = 0
    wanted = col_ids[col_slot]
    source_slot = wanted // grid_rows
    piece_here = lax.dynamic_index_in_dim(arrived, source_slot, 0, keepdims=False)
    col_pieces = [broadcast(piece_here, "row", wanted % grid_rows)]
    panels.append((arrived, col_pieces))
    row_slot = 0
    col_slot = 0
    chosen = jnp.logical_and(row_ids[row_slot] >= col_ids[col_slot], col_ids[col_slot] > 0)
    tiles[row_slot][col_slot] = lax.cond(
        chosen,
        lambda square, rs=row_slot, cs=col_slot, pid=0: apply_panel(square, rs, cs, pid),
        lambda square: square,
        tiles[row_slot][col_slot],
    )
    row_slot = 0
    kept = [jnp.where(row_ids[row_slot] >= col_ids[0], tiles[row_slot][0], 0.0)]
    finished = [jnp.stack(kept, axis=1)]
    stacked = jnp.stack(finished, axis=0)
    return stacked.reshape(tile_rows, 1, tile_order, tile_cols, 1, tile_order)


def solution(mesh):
    return jax.shard_map(
        on_device,
        mesh=mesh,
        in_specs=(P(None, "row", None, None, "col", None), P()),
        out_specs=P(None, "row", None, None, "col", None),
        check_vma=False,
    )
```

profile of v0, /device:TPU:9, one launch (start us, length us, event | category | flops | bytes accessed | tf_op | source)
XLA Modules:
  0.0 705.8 jit_solution(6807811891235126774)
XLA Ops:
  6.5 0.0 all-reduce.4.cloned.1.call-start
  6.5 1.9 fusion.69
  9.1 2.1 bitcast_add_fusion.1
  11.2 10.6 %conditional.3 = (f32[896,896]{1,0:T(8,128)}, f32[896,896]{1,0:T(8,128)}) conditional(s32[]{:T(128)} %convert_element_type.26, () %tuple.28, (f32[896,896]{1,0:T(8,128)S(1)}, f32[896,896]{1,0:T(8,128)}, f32[896,896]{1,0:T(8,128)}, f32[896,896]{1,0:T(8,128)}, f32[896,896]{1,0:T(8,128)}, /*index=5*/f32[896,896]{1,0:T(8,128)}, f32[896,896]{1,0:T(8,128)}, ...), branch_computations={%region_0.1_spmd, %region_1.16_spmd} | conditional | flops 6878954496 | bytes 101458848 | solution.py:67
  11.2 1.9 broadcast.318
  13.2 1.9 broadcast.318.clone
  21.9 1.9 broadcast_select_fusion
  23.8 0.0 all-reduce.4.cloned.1.call-update
  23.8 0.0 all-gather.2.cloned.1.call-start
  23.9 416.9 %all-reduce.4.cloned.1.call-done = f32[896,896]{1,0:T(8,128)} async-done(((f32[896,896]{1,0:T(8,128)}), f32[896,896]{1,0:T(8,128)}) %all-reduce.4.cloned.1.call-update) | async-done | bytes 3211280 | tf_op jit(solution)/shard_map/psum | solution.py:9
  440.8 1.9 conditional.4
  440.8 1.9 squeeze.14
  442.7 2.2 select_select_fusion.1
  444.9 4.7 stack.4
  449.7 53.7 %all_to_all.5 = f32[1,896,896]{2,0,1:T(1,128)S(1)} all-to-all(f32[1,896,896]{2,0,1:T(1,128)S(1)} %stack.4), channel_id=1, replica_groups=mesh['row'=16,'col'=16] {'col'}, dimensions={1} | all-to-all | bytes 6422528 | tf_op jit(solution)/shard_map/all_to_all | solution.py:76
  503.4 0.1 slice.228
  503.4 0.7 copy.10
  504.1 0.0 all-gather.2.cloned.1.call-update
  504.2 0.0 all-reduce.6.cloned.1.call-start
  504.2 49.1 %all-gather.2.cloned.1.call-done = f32[1,896,896]{2,1,0:T(8,128)} async-done(((f32[1,56,896]{2,1,0:T(8,128)}), f32[1,896,896]{2,1,0:T(8,128)}) %all-gather.2.cloned.1.call-update) | async-done | bytes 3211280 | tf_op jit(solution)/shard_map/all_gather | solution.py:80
  553.3 5.3 bitcast_select_fusion
  558.6 0.0 all-reduce.6.cloned.1.call-update
  558.6 119.2 %all-reduce.6.cloned.1.call-done = f32[896,896]{1,0:T(8,128)} async-done(((f32[896,896]{1,0:T(8,128)}), f32[896,896]{1,0:T(8,128)}) %all-reduce.6.cloned.1.call-update) | async-done | bytes 3211280 | tf_op jit(solution)/shard_map/psum | solution.py:9
  677.8 16.0 %conditional.5 = (f32[896,896]{1,0:T(8,128)S(1)}) conditional(s32[]{:T(128)} %convert_element_type.24, f32[896,896]{1,0:T(8,128)S(1)} %get-tuple-element.131, (f32[1,896,896]{2,1,0:T(8,128)}, f32[896,896]{1,0:T(8,128)}, f32[896,896]{1,0:T(8,128)S(1)}) %tuple.31), branch_computations={%region_20.21_spmd, %region_21.22_spmd} | conditional | flops 8632680448 | bytes 12845064 | solution.py:92
  678.2 15.5 %fusion.2 = f32[896,896]{1,0:T(8,128)S(1)} fusion(f32[896,896]{1,0:T(8,128)S(1)} %get-tuple-element.43, f32[896,896]{1,0:T(8,128)} %get-tuple-element.45, f32[1,896,896]{2,1,0:T(8,128)} %get-tuple-element.44), kind=kOutput, calls=%fused_computation.2 | convolution fusion | flops 8632680448 | bytes 12845056 | tf_op jit(solution)/shard_map/cond/branch_1_fun/dot_general | solution.py:13
  693.9 0.2 select_bitcast_fusion.6
  694.1 5.0 copy.8
Async XLA Ops:
  6.5 434.2 %all-reduce.4.cloned.1.call-start = ((), (), s32[]{:S(2)}) async-start(), calls=%async_computation.1 | async-start | bytes 6422528 | tf_op jit(solution)/shard_map/psum | solution.py:9
  23.8 529.5 %all-gather.2.cloned.1.call-start = ((), (), s32[]{:S(2)}) async-start(), calls=%async_computation.2 | async-start | bytes 3411968 | tf_op jit(solution)/shard_map/all_gather | solution.py:80
  504.2 173.7 %all-reduce.6.cloned.1.call-start = ((), (), s32[]{:S(2)}) async-start(), calls=%async_computation.3 | async-start | bytes 6422528 | tf_op jit(solution)/shard_map/psum | solution.py:9
Sparse Core Ops, SparseCore 0:
  23.9 416.7 all-reduce.3
  504.3 48.9 all-gather.1
  558.7 119.0 all-reduce.5
where the time goes:
time: 717 us; the launch traced here: 706 us
  waiting for transfers between devices  585 us (82%)
  blocking collectives  53.7 us (7%)
  local copies, waits for them, and re-layouts  16.2 us (2%)
  matrix products  15.5 us (2%)
  between operations  14 us (2%)
  other arithmetic  13.7 us (2%)
  loops' own time  7.36 us (1%)
    psum x2, waiting for transfers between devices, broadcast(): return lax.psum(jnp.where(mine, array, jnp.zeros_like(array)), axis)  536 us
    all_to_all x1, blocking collectives, on_device(): lax.all_to_all(outgoing, 'col', split_axis=1, concat_axis=1, tiled=True)  53.7 us
    all_gather x1, waiting for transfers between devices, on_device(): arrived = lax.all_gather(home_strip, 'col', axis=1, tiled=True)  49.1 us
    dot_general x1, matrix products, times_transposed(): lax.dot_general(left, right, (((1,), (1,)), ((), ())), precision=lax.Prec...  15.5 us
  transfers between devices with their start and end apart: 3, of which 3 were waited for; matrix products, arithmetic and copies ran while one was open for 0% of the time, Pallas kernels for 0%

commit v1 on v0

--- a/solution.py
+++ b/solution.py
@@ -6,7 +6,7 @@
 
 def broadcast(array, axis, root):
     mine = lax.axis_index(axis) == root
-    return lax.psum(jnp.where(mine, array, jnp.zeros_like(array)), axis)
+    return jnp.sum(lax.all_gather(jnp.where(mine, array, jnp.zeros_like(array)), axis), axis=0)
 
 
 def times_transposed(left, right):

time: 717 us -> 1030 us (1.44)
  waiting for transfers between devices: 585 us -> 857 us
  other arithmetic: 13.7 us -> 57 us
    all_gather x0 -> x2, waiting for transfers between devices: none -> 809 us  [broadcast(): lax.all_gather(jnp.where(mine, array, jnp.zeros_like(array)), axis)]
    psum x2 -> x0, waiting for transfers between devices: 536 us -> none  [broadcast(): return lax.psum(jnp.where(mine, array, jnp.zeros_like(array)), axis)]
    reduce_sum x0 -> x2, other arithmetic: none -> 39 us  [broadcast(): jnp.sum(lax.all_gather(jnp.where(mine, array, jnp.zeros_like(array)), axi...]
where the time goes in v1:
time: 1030 us; the launch traced here: 1020 us
  waiting for transfers between devices  857 us (83%)
  other arithmetic  57 us (6%)
  blocking collectives  54 us (5%)
  local copies, waits for them, and re-layouts  18.1 us (2%)
  matrix products  14.9 us (1%)
  between operations  14.1 us (1%)
    all_gather x2, waiting for transfers between devices, broadcast(): lax.all_gather(jnp.where(mine, array, jnp.zeros_like(array)), axis)  809 us
    all_to_all x1, blocking collectives, on_device(): lax.all_to_all(outgoing, 'col', split_axis=1, concat_axis=1, tiled=True)  54 us
    all_gather x1, waiting for transfers between devices, on_device(): arrived = lax.all_gather(home_strip, 'col', axis=1, tiled=True)  48.3 us
    reduce_sum x2, other arithmetic, broadcast(): jnp.sum(lax.all_gather(jnp.where(mine, array, jnp.zeros_like(array)), axi...  39 us
  transfers between devices with their start and end apart: 3, of which 3 were waited for; matrix products, arithmetic and copies ran while one was open for 0% of the time, Pallas kernels for 0%

profile of v1, /device:TPU:9, one launch (start us, length us, event | category | flops | bytes accessed | tf_op | source)
XLA Modules:
  0.0 1022.9 jit_solution(8562571703228158040)
XLA Ops:
  6.5 0.0 all-gather.9.cloned.1.call-start
  6.5 1.9 fusion.69
  9.1 2.1 bitcast_add_fusion.1
  11.2 11.3 %conditional.3 = (f32[896,896]{1,0:T(8,128)}, f32[896,896]{1,0:T(8,128)}) conditional(s32[]{:T(128)} %convert_element_type.26, () %tuple.28, (f32[896,896]{1,0:T(8,128)S(1)}, f32[896,896]{1,0:T(8,128)}, f32[896,896]{1,0:T(8,128)}, f32[896,896]{1,0:T(8,128)}, f32[896,896]{1,0:T(8,128)}, /*index=5*/f32[896,896]{1,0:T(8,128)}, f32[896,896]{1,0:T(8,128)}, ...), branch_computations={%region_0.1_spmd, %region_1.16_spmd} | conditional | flops 6878954496 | bytes 101458848 | solution.py:67
  11.2 1.9 broadcast.321
  13.2 1.9 broadcast.321.clone
  22.6 1.9 broadcast_select_fusion.1
  24.5 0.0 all-gather.9.cloned.1.call-update
  24.5 0.0 all-gather.5.cloned.1.call-start
  24.5 556.3 %all-gather.9.cloned.1.call-done = f32[14336,896]{1,0:T(8,128)} async-done(((f32[896,896]{1,0:T(8,128)}), f32[14336,896]{1,0:T(8,128)}) %all-gather.9.cloned.1.call-update) | async-done | bytes 51380240 | tf_op jit(solution)/shard_map/all_gather | solution.py:9
  580.8 19.5 %reduce_sum.18 = f32[896,896]{1,0:T(8,128)} reduce(f32[16,896,896]{2,1,0:T(8,128)} %bitcast.108, f32[]{:T(128)} %constant.283.clone.1), dimensions={0}, to_apply=%region_16.17 | reduce | flops 12042240 | bytes 54591492 | tf_op jit(solution)/shard_map/reduce_sum | solution.py:9
  600.3 1.9 conditional.4
  600.3 1.9 squeeze.14
  602.1 2.2 select_select_fusion.1
  604.4 4.7 stack.4
  609.1 54.0 %all_to_all.5 = f32[1,896,896]{2,0,1:T(1,128)S(1)} all-to-all(f32[1,896,896]{2,0,1:T(1,128)S(1)} %stack.4), channel_id=1, replica_groups=mesh['row'=16,'col'=16] {'col'}, dimensions={1} | all-to-all | bytes 6422528 | tf_op jit(solution)/shard_map/all_to_all | solution.py:76
  663.1 0.1 slice.228
  663.1 0.7 copy.10
  663.8 0.0 all-gather.5.cloned.1.call-update
  663.9 0.0 all-gather.7.cloned.1.call-start
  663.9 48.3 %all-gather.5.cloned.1.call-done = f32[1,896,896]{2,1,0:T(8,128)} async-done(((f32[1,56,896]{2,1,0:T(8,128)}), f32[1,896,896]{2,1,0:T(8,128)}) %all-gather.5.cloned.1.call-update) | async-done | bytes 3211280 | tf_op jit(solution)/shard_map/all_gather | solution.py:80
  712.2 3.8 broadcast_select_fusion
  716.0 0.0 copy-start
  716.0 0.0 all-gather.7.cloned.1.call-update
  716.0 1.9 copy-done
  717.9 3.9 bitcast_select_fusion
  721.8 252.8 %all-gather.7.cloned.1.call-done = f32[16,896,896]{2,1,0:T(8,128)} async-done(((f32[1,896,896]{2,1,0:T(8,128)}), f32[16,896,896]{2,1,0:T(8,128)}) %all-gather.7.cloned.1.call-update) | async-done | bytes 51380240 | tf_op jit(solution)/shard_map/all_gather | solution.py:9
  974.6 19.5 %reduce_sum.19 = f32[896,896]{1,0:T(8,128)} reduce(f32[16,896,896]{2,1,0:T(8,128)} %all-gather.7.cloned.1.call-done, f32[]{:T(128)} %constant.283.clone.1), dimensions={0}, to_apply=%region_19.20 | reduce | flops 12042240 | bytes 54591492 | tf_op jit(solution)/shard_map/reduce_sum | solution.py:9
  994.1 14.9 %conditional.5 = (f32[896,896]{1,0:T(8,128)}) conditional(s32[]{:T(128)} %convert_element_type.24, f32[896,896]{1,0:T(8,128)} %bitcast_select_fusion, (f32[1,896,896]{2,1,0:T(8,128)S(1)}, f32[896,896]{1,0:T(8,128)}, f32[896,896]{1,0:T(8,128)}) %tuple.93), branch_computations={%region_20.21_spmd, %region_21.22_spmd} | conditional | flops 8632680448 | bytes 12845064 | solution.py:92
  994.1 14.9 %fusion.2 = f32[896,896]{1,0:T(8,128)} fusion(f32[896,896]{1,0:T(8,128)} %get-tuple-element.43, f32[896,896]{1,0:T(8,128)} %get-tuple-element.45, f32[1,896,896]{2,1,0:T(8,128)S(1)} %get-tuple-element.44), kind=kOutput, calls=%fused_computation.2 | convolution fusion | flops 8632680448 | bytes 12845056 | tf_op jit(solution)/shard_map/cond/branch_1_fun/dot_general | solution.py:13
  1009.1 2.1 select_bitcast_fusion.6
  1011.2 5.0 copy.8
Async XLA Ops:
  6.5 574.3 %all-gather.9.cloned.1.call-start = ((), (), s32[]{:S(2)}) async-start(), calls=%async_computation.3 | async-start | bytes 54591488 | tf_op jit(solution)/shard_map/all_gather | solution.py:9
  24.5 687.7 %all-gather.5.cloned.1.call-start = ((), (), s32[]{:S(2)}) async-start(), calls=%async_computation.1 | async-start | bytes 3411968 | tf_op jit(solution)/shard_map/all_gather | solution.py:80
  663.9 310.8 %all-gather.7.cloned.1.call-start = ((), (), s32[]{:S(2)}) async-start(), calls=%async_computation.2 | async-start | bytes 54591488 | tf_op jit(solution)/shard_map/all_gather | solution.py:9
  716.0 1.9 copy-start
Sparse Core Ops, SparseCore 0:
  24.6 556.1 all-gather.8
  664.0 48.1 all-gather.4
  716.1 258.4 all-gather.6
